TPU v7x, 32 devices: a whole 2x2x4 slice. The times are simulated.
32 devices in a mesh: body: 2 (over core), gx: 4 (over z), gy: 4 (over y, x).
Axes of the slice: x: 2, y: 2, z: 4, core: 2. Of those that a mesh axis runs over, the one named last changes fastest.
Arguments:
- disp: float32 [2, 3, 32, 128, 128], P('body', None, 'gx', 'gy'), may hold values from -4 to 4
- force: float32 [2, 3, 32, 128, 128], P('body', None, 'gx', 'gy'), may hold values from -12 to 12
- kappa: float32 [2, 32, 128, 128], P('body', 'gx', 'gy'), may hold values from 0.05 to 0.5
- sigma: float32 [2, 32, 128, 128], P('body', 'gx', 'gy'), may hold values from 0.2 to 1
- gap0: float32 [32, 128], P(('gx', 'gy')), may hold values from -3 to 3
- pressure: float32 [32, 128], P(('gx', 'gy')), may hold values from 0 to 1
- mortar: float32 [32, 128, 128], P(('gx', 'gy')), may hold values from -0.5 to 0.5
- partner: int32 [32], P(('gx', 'gy')), may hold values from 0 to 7
- active: int32 [32], P(('gx', 'gy')), may hold values 0 or 1
Outputs:
- increment: float32 [2, 3, 32, 128, 128], P('body', None, 'gx', 'gy')
- new_pressure: float32 [32, 128], P(('gx', 'gy'))
Inputs may be any that keep to these rules, and one draw needn't show every extreme that they name: partner numbers a master block of the same gy index: gx index times 2 plus the local block. 1 marks a block of the active contact set.
All inputs are finite; a program needn't handle non-finite values.
Results may differ from a plain program's by a relative error of at most 0.00015.
Values sent between devices are 32-bit elements; how exact they have to be, the bound alone decides.
A program may use at most 64 MiB of HBM per device.

v0:
```python
import functools

import jax
import jax.numpy as jnp
from jax import lax
from jax.experimental import pallas as pl
from jax.experimental.pallas import tpu as pltpu
from jax.sharding import PartitionSpec as P

MESH = pl.DeviceIdType.MESH
YB = 8
DIRS = tuple((dx, dy) for dx in (-1, 0, 1) for dy in (-1, 0, 1) if dx != 0 or dy != 0)


def kernel(nb, ngx, ngy, disp, force, kappa, sigma, gap0_in, press_in, mortar, partner_in, active_in,
           inc_out, np_out, gap0, press, partner, active, f0, f1, f2, v2, diag, force_v, sigma_v, mort, surf, usend, urecv,
           final, cols, load_sem, hs, hr, ss, sr, us, ur, fs, fr):
    comp, cx, cy, nz = force_v.shape
    bpd, sblk = gap0.shape
    per = sblk // cy
    b = lax.axis_index("body")
    gx = lax.axis_index("gx")
    gy = lax.axis_index("gy")

    loads = [
        pltpu.make_async_copy(disp.at[0], f0.at[pl.ds(0, comp), pl.ds(1, cx), pl.ds(YB, cy)], load_sem.at[0]),
        pltpu.make_async_copy(kappa.at[0], f0.at[comp, pl.ds(1, cx), pl.ds(YB, cy)], load_sem.at[1]),
        pltpu.make_async_copy(mortar, mort, load_sem.at[2]),
        pltpu.make_async_copy(sigma.at[0], sigma_v, load_sem.at[3]),
        pltpu.make_async_copy(force.at[0], force_v, load_sem.at[4]),
        pltpu.make_async_copy(gap0_in, gap0, load_sem.at[5]),
        pltpu.make_async_copy(press_in, press, load_sem.at[6]),
        pltpu.make_async_copy(partner_in, partner, load_sem.at[7]),
        pltpu.make_async_copy(active_in, active, load_sem.at[8]),
    ]
    for load in loads:
        load.start()

    def exists(dx, dy):
        good = jnp.bool_(True)
        if dx < 0:
            good = good & (gx >= 1)
        if dx > 0:
            good = good & (gx < ngx - 1)
        if dy < 0:
            good = good & (gy >= 1)
        if dy > 0:
            good = good & (gy < ngy - 1)
        return good

    row_peers = [(db, k) for db in range(nb) for k in range(ngx) if db or k]
    count = nb * ngx * ngy
    me = (b * ngx + gx) * ngy + gy

    def place_of(other):
        return {"body": other // (ngx * ngy), "gx": lax.rem(other // ngy, ngx), "gy": lax.rem(other, ngy)}

    def each_peer(act):
        if count <= 64:
            for k in range(1, count):
                act(k)
        else:
            pl.loop(1, count)(act)

    barrier = pltpu.get_barrier_semaphore()
    if ngy <= 4:
        for db, k in row_peers:
            pl.semaphore_signal(barrier, inc=1, device_id={"body": lax.rem(b + db, nb), "gx": lax.rem(gx + k, ngx)},
                                device_id_type=MESH)
        expect = len(row_peers)
        for dx, dy in DIRS:
            if dy:
                here = exists(dx, dy)
                expect = expect + here.astype(jnp.int32)

                @pl.when(here)
                def _():
                    pl.semaphore_signal(barrier, inc=1, device_id={"gx": gx + dx, "gy": gy + dy}, device_id_type=MESH)
    else:
        each_peer(lambda k: pl.semaphore_signal(barrier, inc=1, device_id=place_of(lax.rem(me + k, count)),
                                                device_id_type=MESH))
        expect = count - 1

    for side, x in ((-1, 0), (1, cx + 1)):
        @pl.when(jnp.logical_not(exists(side, 0)))
        def _():
            for f in (f0, f1, f2):
                for c in range(f.shape[0]):
                    f[c, x, YB - 1 : YB] = jnp.zeros((1, nz), f.dtype)
                    f[c, x, YB : YB + cy] = jnp.zeros((cy, nz), f.dtype)
                    f[c, x, YB + cy : YB + cy + 1] = jnp.zeros((1, nz), f.dtype)
    for side, y in ((-1, YB - 1), (1, YB + cy)):
        @pl.when(jnp.logical_not(exists(0, side)))
        def _():
            for f in (f0, f1, f2):
                for c in range(f.shape[0]):
                    for x in range(cx + 2):
                        f[c, x, y : y + 1] = jnp.zeros((1, nz), f.dtype)

    lane = lax.broadcasted_iota(jnp.int32, (sblk, nz), 1)
    eye = lax.broadcasted_iota(jnp.int32, (sblk, nz), 0) == lane
    first_lane = lane == 0
    lane_row = lax.broadcasted_iota(jnp.int32, (cy, nz), 1)
    left_w = jnp.where(lane_row == 0, 0.0, 0.5)
    right_w = jnp.where(lane_row == nz - 1, 0.0, 0.5)

    def to_col(row):
        return jnp.sum(jnp.where(eye, row, 0.0), axis=1, keepdims=True)

    def to_row(col):
        return jnp.sum(jnp.where(eye, col, 0.0), axis=0, keepdims=True)

    def tz(v):
        return v + left_w * pltpu.roll(v, 1, 1) + right_w * pltpu.roll(v, nz - 1, 1)

    def surface_rows(f, r):
        for l in range(bpd):
            block = f[comp - 1, 1 + l * per : 1 + (l + 1) * per, YB : YB + cy, :].reshape(sblk, nz)
            surf[r, b, gx, l : l + 1, :] = to_row(block[:, 0:1])

    pending = []

    def halo_copy(f, r, d, dx, dy, sending):
        def part(delta, size, base):
            if delta == 0:
                return pl.ds(base, size), pl.ds(base, size)
            if delta < 0:
                return pl.ds(base, 1), pl.ds(base + size, 1)
            return pl.ds(base + size - 1, 1), pl.ds(base - 1, 1)
        sx, tx = part(dx, cx, 1)
        sy, ty = part(dy, cy, YB)
        allc = pl.ds(0, f.shape[0])
        return pltpu.make_async_remote_copy(
            src_ref=f.at[allc, sx, sy], dst_ref=f.at[allc, tx, ty], send_sem=hs.at[r, d], recv_sem=hr.at[r, d],
            device_id={"gx": gx + dx, "gy": gy + dy}, device_id_type=MESH)

    def halo_send(f, r):
        for d, (dx, dy) in enumerate(DIRS):
            @pl.when(exists(dx, dy))
            def _():
                halo_copy(f, r, d, dx, dy, True).start()

    def halo_wait(f, r):
        for d, (dx, dy) in enumerate(DIRS):
            @pl.when(exists(-dx, -dy))
            def _():
                halo_copy(f, r, d, dx, dy, False).wait_recv()

    def halo_done(f, r):
        for d, (dx, dy) in enumerate(DIRS):
            @pl.when(exists(dx, dy))
            def _():
                halo_copy(f, r, d, dx, dy, True).wait_send()

    def surf_copy(r, i, db, k, incoming):
        ob, og = lax.rem(b + db, nb), lax.rem(gx + k, ngx)
        wb, wg = (ob, og) if incoming else (b, gx)
        return pltpu.make_async_remote_copy(
            src_ref=surf.at[r, wb, wg], dst_ref=surf.at[r, wb, wg], send_sem=ss.at[r, i],
            recv_sem=sr.at[r, wb * ngx + wg], device_id={"body": ob, "gx": og}, device_id_type=MESH)

    def surf_each(r, incoming, act):
        for i, (db, k) in enumerate(row_peers):
            def go():
                act(surf_copy(r, i, db, k, incoming))
            if db == 1 and k == 0:
                go()
            else:
                origin = lax.rem(b + db, nb) if incoming else b
                pl.when(origin == 1)(go)

    def surf_send(r):
        surf_each(r, False, lambda copy: copy.start())

    def surf_wait(r):
        surf_each(r, True, lambda copy: copy.wait_recv())

    def u_copy(r, k, incoming):
        og = lax.rem(gx + k, ngx)
        return pltpu.make_async_remote_copy(
            src_ref=usend.at[r, og], dst_ref=urecv.at[r, og if incoming else gx], send_sem=us.at[r, k],
            recv_sem=ur.at[r, og if incoming else gx], device_id={"gx": og}, device_id_type=MESH)

    def final_copy(k, incoming):
        other = lax.rem(me + k, count)
        w = other if incoming else me
        return pltpu.make_async_remote_copy(
            src_ref=final.at[w], dst_ref=final.at[w], send_sem=fs.at[k], recv_sem=fr.at[w],
            device_id=place_of(other),
            device_id_type=MESH)

    def b_of(r, l):
        picked = jnp.zeros((1, sblk), jnp.float32)
        for g in range(ngx):
            for q in range(bpd):
                picked = picked + jnp.where(partner[l] == g * bpd + q, surf[r, 1, g, q : q + 1, :], 0.0)
        slave = surf[r, 0, gx, l : l + 1, :]
        return -jnp.sum(mort[l] * picked + jnp.where(eye, slave, 0.0), axis=1, keepdims=True)

    def u_start(r):
        pulled = [jnp.sum(mort[l] * cols[5, l], axis=0, keepdims=True) for l in range(bpd)]
        for g in range(ngx):
            for q in range(bpd):
                row = jnp.zeros((1, sblk), jnp.float32)
                for l in range(bpd):
                    row = row + jnp.where(partner[l] == g * bpd + q, pulled[l], 0.0)
                usend[r, g, q : q + 1, :] = row

        @pl.when(b == 1)
        def _():
            for k in range(1, ngx):
                u_copy(r, k, False).start()

    def u_finish(r, f):
        def add(l, col):
            xs = slice(1 + l * per, 1 + (l + 1) * per)
            block = f[comp - 1, xs, YB : YB + cy, :].reshape(sblk, nz)
            f[comp - 1, xs, YB : YB + cy, :] = (block - jnp.where(first_lane, col, 0.0)).reshape(per, cy, nz)

        @pl.when(b == 0)
        def _():
            for l in range(bpd):
                add(l, cols[5, l])

        @pl.when(b == 1)
        def _():
            for k in range(1, ngx):
                u_copy(r, k, True).wait_recv()
            urecv[r, gx] = usend[r, gx]
            for l in range(bpd):
                row = urecv[r, 0, l : l + 1, :]
                for g in range(1, ngx):
                    row = row + urecv[r, g, l : l + 1, :]
                add(l, to_col(row))

    def apply(f, emit):
        @pl.loop(0, comp)
        def _(c):
            window = []
            for x in range(cx + 2):
                kap = [f0[comp, x, YB + s : YB + s + cy, :] for s in (-1, 0, 1)]
                val = [f[c, x, YB + s : YB + s + cy, :] for s in (-1, 0, 1)]
                window.append((val[1] + 0.5 * (val[0] + val[2]),
                               kap[1] * val[1] + 0.5 * (kap[0] * val[0] + kap[2] * val[2])))
                if x >= 2:
                    p = window[x - 1][0] + 0.5 * (window[x - 2][0] + window[x][0])
                    q = window[x - 1][1] + 0.5 * (window[x - 2][1] + window[x][1])
                    k0 = f0[comp, x - 1, YB : YB + cy, :]
                    v0 = f[c, x - 1, YB : YB + cy, :]
                    emit(c, x - 2, diag[x - 2] * v0 - k0 * tz(p) - tz(q))

    loads[0].wait()
    loads[1].wait()
    surface_rows(f0, 0)
    pl.semaphore_wait(barrier, expect)

    surf_send(0)
    halo_send(f0, 0)
    for load in loads[2:]:
        load.wait()
    surf_wait(0)
    for l in range(bpd):
        gap = to_col(gap0[l : l + 1, :]) + b_of(0, l)
        prs = to_col(press[l : l + 1, :])
        radius = jnp.sqrt(gap * gap + prs * prs + 0.01)
        per_radius = 1.0 / radius
        complement = gap + prs - radius
        per_divisor = 1.0 / ((1.0 - prs * per_radius) + 0.5)
        flag = active[l].astype(jnp.float32)
        cols[1, l] = complement * per_divisor
        cols[2, l] = (1.0 - gap * per_radius) * per_divisor
        cols[5, l] = flag * (prs - complement * per_divisor)
    u_start(0)
    for l in range(bpd):
        cols[0, l] = active[l].astype(jnp.float32) * cols[2, l]
    halo_wait(f0, 0)
    window = []
    for x in range(cx + 2):
        kap = [f0[comp, x, YB + s : YB + s + cy, :] for s in (-1, 0, 1)]
        window.append(kap[1] + 0.5 * (kap[0] + kap[2]))
        if x >= 2:
            p = window[x - 1] + 0.5 * (window[x - 2] + window[x])
            diag[x - 2] = sigma_v[x - 2] + 8.0 * f0[comp, x - 1, YB : YB + cy, :] + tz(p)

    def emit_rhs(c, x, val):
        f1[c, 1 + x, YB : YB + cy, :] = force_v[c, x] - val

    apply(f0, emit_rhs)
    u_finish(0, f1)

    surface_rows(f1, 1)
    surf_send(1)
    halo_send(f1, 1)
    surf_wait(1)
    for l in range(bpd):
        gap = b_of(1, l)
        cols[3, l] = gap
        cols[5, l] = cols[0, l] * gap
    u_start(1)
    halo_wait(f1, 1)

    def emit_v1(c, x, val):
        f2[c, 1 + x, YB : YB + cy, :] = val

    apply(f1, emit_v1)

    def sum_of(left, right):
        total = jnp.zeros((cy, nz), jnp.float32)
        for c in range(comp):
            for x in range(cx):
                total = total + left(c, x) * right(c, x)
        return jnp.sum(jnp.sum(total, axis=0, keepdims=True), axis=1, keepdims=True)

    slave_side = (b == 0).astype(jnp.float32)

    def contact_sum(left, right):
        total = jnp.zeros((1, 1), jnp.float32)
        for l in range(bpd):
            total = total + jnp.sum(cols[0, l] * left(l) * right(l), axis=0, keepdims=True)
        return slave_side * total

    def r0_of(c, x):
        return f1[c, 1 + x, YB : YB + cy, :]

    def v1_of(c, x):
        return f2[c, 1 + x, YB : YB + cy, :]

    u_finish(1, f2)

    surface_rows(f2, 2)
    surf_send(2)
    halo_send(f2, 2)
    rr = sum_of(r0_of, r0_of)
    rv = sum_of(r0_of, v1_of)
    vv = sum_of(v1_of, v1_of)
    own = jnp.where(vv > 0.0, rv / jnp.where(vv > 0.0, vv, 1.0), 0.0)

    def near_of(c, x):
        return r0_of(c, x) - own * v1_of(c, x)

    nn = sum_of(near_of, near_of)
    nv = sum_of(near_of, v1_of)
    surf_wait(2)
    for l in range(bpd):
        cols[4, l] = b_of(2, l)
    halo_wait(f2, 2)

    def emit_v2(c, x, val):
        v2[c, x] = val

    apply(f2, emit_v2)
    nw = sum_of(near_of, lambda c, x: v2[c, x]) + contact_sum(lambda l: cols[3, l] - own * cols[4, l], lambda l: cols[4, l])
    vw = sum_of(v1_of, lambda c, x: v2[c, x]) + contact_sum(lambda l: cols[4, l], lambda l: cols[4, l])

    lane_of = lax.broadcasted_iota(jnp.int32, (1, sblk), 1)
    packed = jnp.zeros((1, sblk), jnp.float32)
    for i, number in enumerate((rr, rv, vv, nn, nv, nw, vw, own)):
        packed = jnp.where(lane_of == i, number, packed)
    final[me] = packed
    each_peer(lambda k: final_copy(k, False).start())
    for r, f in enumerate((f0, f1, f2)):
        halo_done(f, r)
    for r in range(3):
        surf_each(r, False, lambda copy: copy.wait_send())
    @pl.when(b == 1)
    def _():
        for r in range(2):
            for k in range(1, ngx):
                u_copy(r, k, False).wait_send()

    each_peer(lambda k: final_copy(k, True).wait_recv())
    table = final[...].reshape(count, sblk)

    def over(act):
        return jnp.sum(act(*[table[:, i : i + 1] for i in range(8)]), axis=0, keepdims=True)

    norm0 = over(lambda rr, rv, vv, nn, nv, nw, vw, own: rr)
    alpha0 = norm0 / over(lambda rr, rv, vv, nn, nv, nw, vw, own: rv)
    norm1 = over(lambda rr, rv, vv, nn, nv, nw, vw, own: nn - (alpha0 - own) * (2.0 * nv - (alpha0 - own) * vv))
    product1 = over(lambda rr, rv, vv, nn, nv, nw, vw, own:
                    nv - (alpha0 - own) * vv - alpha0 * (nw - (alpha0 - own) * vw))
    ratio = norm1 / norm0
    alpha1 = norm1 / (product1 - ratio * norm1 / alpha0)
    coef_r = alpha0 + alpha1 * (1.0 + ratio)
    coef_v = -alpha1 * alpha0
    for c in range(comp):
        for x in range(cx):
            inc_out[0, c, x] = coef_r * r0_of(c, x) + coef_v * v1_of(c, x)
    for l in range(bpd):
        change = coef_r * cols[3, l] + coef_v * cols[4, l]
        flag = active[l].astype(jnp.float32)
        step = to_row(cols[1, l] + cols[2, l] * change)
        np_out[l : l + 1, :] = flag * (press[l : l + 1, :] - step)
    each_peer(lambda k: final_copy(k, False).wait_send())


def on_device(disp, force, kappa, sigma, gap0, pressure, mortar, partner, active):
    nb, ngx, ngy = (lax.axis_size(a) for a in ("body", "gx", "gy"))
    _, comp, cx, cy, nz = disp.shape
    bpd, sblk, _ = mortar.shape
    f32 = jnp.float32
    any_spec = pl.BlockSpec(memory_space=pl.ANY)
    vmem = pl.BlockSpec(memory_space=pltpu.VMEM)
    rows = cy + 2 * YB
    dma = pltpu.SemaphoreType.DMA
    return pl.pallas_call(
        functools.partial(kernel, nb, ngx, ngy),
        out_shape=(pltpu.VMEM(disp.shape, f32), pltpu.VMEM(gap0.shape, f32)),
        in_specs=[any_spec] * 9,
        out_specs=(vmem, vmem),
        scratch_shapes=[
            pltpu.VMEM((bpd, sblk), f32),
            pltpu.VMEM((bpd, sblk), f32),
            pltpu.SMEM((bpd,), jnp.int32),
            pltpu.SMEM((bpd,), jnp.int32),
            pltpu.VMEM((comp + 1, cx + 2, rows, nz), f32),
            pltpu.VMEM((comp, cx + 2, rows, nz), f32),
            pltpu.VMEM((comp, cx + 2, rows, nz), f32),
            pltpu.VMEM((comp, cx, cy, nz), f32),
            pltpu.VMEM((cx, cy, nz), f32),
            pltpu.VMEM((comp, cx, cy, nz), f32),
            pltpu.VMEM((cx, cy, nz), f32),
            pltpu.VMEM((bpd, sblk, sblk), f32),
            pltpu.VMEM((3, nb, ngx, bpd, sblk), f32),
            pltpu.VMEM((2, ngx, bpd, sblk), f32),
            pltpu.VMEM((2, ngx, bpd, sblk), f32),
            pltpu.VMEM((nb * ngx * ngy, 1, sblk), f32),
            pltpu.VMEM((6, bpd, sblk, 1), f32),
            dma((9,)),
            dma((3, len(DIRS))), dma((3, len(DIRS))),
            dma((3, nb * ngx)), dma((3, nb * ngx)),
            dma((2, ngx)), dma((2, ngx)),
            dma((nb * ngx * ngy,)), dma((nb * ngx * ngy,)),
        ],
        compiler_params=pltpu.CompilerParams(collective_id=0, has_side_effects=True,
                                             vmem_limit_bytes=60 * 1024 * 1024),
        name="newton_step",
    )(disp, force, kappa, sigma, gap0, pressure, mortar, partner, active)


def solution(mesh):
    placed = (
        P("body", None, "gx", "gy", None),
        P("body", None, "gx", "gy", None),
        P("body", "gx", "gy", None),
        P("body", "gx", "gy", None),
        P(("gx", "gy"), None),
        P(("gx", "gy"), None),
        P(("gx", "gy"), None, None),
        P(("gx", "gy")),
        P(("gx", "gy")),
    )
    return jax.shard_map(
        on_device,
        mesh=mesh,
        in_specs=placed,
        out_specs=(P("body", None, "gx", "gy", None), P(("gx", "gy"), None)),
        check_vma=False,
    )
```

profile of v0, /device:TPU:0, one launch (start us, length us, event | category | flops | bytes accessed | tf_op | source)
XLA Modules:
  0.0 30.2 jit_solution(3672864587801687180)
XLA Ops:
  0.6 28.2 %newton_step.1 = (f32[1,3,8,32,128]{4,3,2,1,0:T(8,128)S(1)}, f32[2,128]{1,0:T(2,128)S(1)}) custom-call(f32[1,3,8,32,128]{4,3,2,1,0:T(8,128)} %disp.1, f32[1,3,8,32,128]{4,3,2,1,0:T(8,128)} %force.1, f32[1,8,32,128]{3,2,1,0:T(8,128)} %kappa.1, f32[1,8,32,128]{3,2,1,0:T(8,128)} %sigma.1, f32[2,128]{1,0:T(2,128)} %gap0_in.1, f32[2,128]{1,0:T(2,128)} %press_in.1, ...), custom_call_target="tpu_custom_call" | custom-call | tf_op jit(solution)/shard_map/newton_step/pallas_call | solution.py:406
  28.9 0.7 %copy.13 = f32[1,3,8,32,128]{4,3,2,1,0:T(8,128)} copy(f32[1,3,8,32,128]{4,3,2,1,0:T(8,128)S(1)} %get-tuple-element.2) | data formatting | bytes 786432
  29.6 0.6 %copy.14 = f32[2,128]{1,0:T(2,128)} copy(f32[2,128]{1,0:T(2,128)S(1)} %get-tuple-element.3) | data formatting | bytes 2048
where the time goes:
time: 30.3 us; the launch traced here: 30.2 us
  Pallas kernels  28.2 us (93%)
  local copies, waits for them, and re-layouts  1.31 us (4%)
  between operations  0.64 us (2%)
    pallas_call x1, Pallas kernels, on_device(): pl.pallas_call(functools.partial(kernel, nb, ngx, ngy), out_shape=(pltpu....  28.2 us
    unnamed x2, local copies, waits for them, and re-layouts  1.31 us

commit v1 on v0

v1 whole, which is shorter than its diff:
```python
import functools

import jax
import jax.numpy as jnp
from jax import lax
from jax.experimental import pallas as pl
from jax.experimental.pallas import tpu as pltpu
from jax.sharding import PartitionSpec as P

MESH = pl.DeviceIdType.MESH
YB = 8
CORNERS = tuple((dx, dy) for dx in (-1, 1) for dy in (-1, 1))
DIRS = CORNERS + ((0, -1), (0, 1), (-1, 0), (1, 0))
RR, RV, VV, NN, NV, NW, VW, OWN = range(8)


def kernel(nb, ngx, ngy, disp, force, kappa, sigma, gap0_in, press_in, mortar, partner_in, active_in,
           r0_out, v1_out, coef, npr_out,
           gap0, press, partner, active, f0, f1, f2, npr, diag, force_v, sigma_v, mort, s1b, pbuf, ub, base, prs_f, t_f, ex_f, sl_f,
           st_f, gr_f, gv_f, acc, own_ref, final, dummy,
           ls, hr, hs, sr, ss, pr, pn, ps, nps, fin):
    comp, cx, cy, nz = force_v.shape
    bpd, sblk = gap0.shape
    per = sblk // cy
    rowblk = ngx * bpd
    last = comp - 1
    b = lax.axis_index("body")
    gx = lax.axis_index("gx")
    gy = lax.axis_index("gy")
    count = nb * ngx * ngy
    me = (b * ngx + gx) * ngy + gy
    f32 = jnp.float32

    def far(at, k, size):
        if size & (size - 1):
            return lax.rem(at + k, size)
        for bit in (1 << i for i in range(size.bit_length() - 1)):
            if k & bit:
                at = at + bit - 2 * bit * lax.rem(at // bit, 2)
        return at

    def place_of(other):
        return {"body": other // (ngx * ngy), "gx": lax.rem(other // ngy, ngx), "gy": lax.rem(other, ngy)}

    def each_peer(act):
        if count <= 64:
            for k in range(1, count):
                act(k)
        else:
            pl.loop(1, count)(act)

    def exists(dx, dy):
        good = jnp.bool_(True)
        if dx < 0:
            good = good & (gx >= 1)
        if dx > 0:
            good = good & (gx < ngx - 1)
        if dy < 0:
            good = good & (gy >= 1)
        if dy > 0:
            good = good & (gy < ngy - 1)
        return good

    def as_int(flag):
        return flag.astype(jnp.int32)

    nys = as_int(exists(0, -1)) + as_int(exists(0, 1))
    nxs = as_int(exists(-1, 0)) + as_int(exists(1, 0))

    def sides(size):
        return (0,) if size == 1 else (1,) if size == 2 else (1, 2)

    def wait_rows(sem, rows):
        part = dummy.at[pl.ds(0, rows)]
        pltpu.make_async_copy(part, part, sem).wait()

    def wait_halo(sem, comps):
        for a in sides(ngx):
            for c in sides(ngy):
                rows = comps * (a * cy + c * cx + a * c)
                if rows:
                    pl.when((nxs == a) & (nys == c))(lambda: wait_rows(sem, rows))

    barrier = pltpu.get_barrier_semaphore()
    if ngy <= 4:
        expect = jnp.where(b == 1, ngx, 0)
        for dx, dy in DIRS:
            here = exists(dx, dy)
            expect = expect + as_int(here)

            @pl.when(here)
            def _():
                pl.semaphore_signal(barrier, inc=1, device_id={"gx": gx + dx, "gy": gy + dy}, device_id_type=MESH)
        for g in range(ngx):
            @pl.when(b == 0)
            def _():
                pl.semaphore_signal(barrier, inc=1, device_id={"body": 1, "gx": g}, device_id_type=MESH)
    else:
        each_peer(lambda k: pl.semaphore_signal(barrier, inc=1, device_id=place_of(lax.rem(me + k, count)),
                                                device_id_type=MESH))
        expect = count - 1

    inner = (pl.ds(1, cx), pl.ds(YB, cy))
    pltpu.make_async_copy(disp.at[0, last], f0.at[(last,) + inner], ls.at[0]).start()
    pltpu.make_async_copy(disp.at[0, pl.ds(0, last)], f0.at[(pl.ds(0, last),) + inner], ls.at[1]).start()
    pltpu.make_async_copy(kappa.at[0], f0.at[(comp,) + inner], ls.at[1]).start()
    pltpu.make_async_copy(gap0_in, gap0, ls.at[3]).start()
    pltpu.make_async_copy(press_in, press, ls.at[3]).start()
    pltpu.make_async_copy(partner_in, partner, ls.at[4]).start()
    pltpu.make_async_copy(active_in, active, ls.at[5]).start()
    pltpu.make_async_copy(mortar, mort, ls.at[6]).start()
    pltpu.make_async_copy(sigma.at[0], sigma_v, ls.at[2]).start()
    pltpu.make_async_copy(force.at[0], force_v, ls.at[2]).start()

    for side, x in ((-1, 0), (1, cx + 1)):
        @pl.when(jnp.logical_not(exists(side, 0)))
        def _():
            for f in (f0, f1, f2):
                for c in range(f.shape[0]):
                    f[c, x, YB - 1 : YB] = jnp.zeros((1, nz), f32)
                    f[c, x, YB : YB + cy] = jnp.zeros((cy, nz), f32)
                    f[c, x, YB + cy : YB + cy + 1] = jnp.zeros((1, nz), f32)
    for side, y in ((-1, YB - 1), (1, YB + cy)):
        @pl.when(jnp.logical_not(exists(0, side)))
        def _():
            for f in (f0, f1, f2):
                for c in range(f.shape[0]):
                    for x in range(cx + 2):
                        f[c, x, y : y + 1] = jnp.zeros((1, nz), f32)
            for g in range(ngx):
                for k in range(3):
                    for l in range(bpd):
                        pbuf[1 + side, g, k, l] = jnp.zeros((1, sblk), f32)
    for d in range(3):
        for q in (0, rowblk + 1):
            ub[d, q] = jnp.zeros((1, sblk), f32)
    for k in range(8):
        acc[k] = jnp.zeros((8, nz), f32)

    lane = lax.broadcasted_iota(jnp.int32, (sblk, nz), 1)
    eye = lax.broadcasted_iota(jnp.int32, (sblk, nz), 0) == lane
    first_lane = lane == 0
    lane_row = lax.broadcasted_iota(jnp.int32, (cy, nz), 1)
    left_w = jnp.where(lane_row == 0, 0.0, 0.5)
    right_w = jnp.where(lane_row == nz - 1, 0.0, 0.5)
    lane_one = lax.broadcasted_iota(jnp.int32, (1, nz), 1)
    block_of = lax.broadcasted_iota(jnp.int32, (rowblk, sblk), 0)
    block_f = block_of.astype(f32)

    def to_full(row):
        return jnp.broadcast_to(jnp.sum(jnp.where(eye, row, 0.0), axis=1, keepdims=True), (sblk, nz))

    def to_row(full):
        return jnp.sum(jnp.where(eye, full, 0.0), axis=0, keepdims=True)

    def tz(v):
        return v + left_w * pltpu.roll(v, 1, 1) + right_w * pltpu.roll(v, nz - 1, 1)

    def block(f, l):
        return f[last, 1 + l * per : 1 + (l + 1) * per, YB : YB + cy, :].reshape(sblk, nz)

    def first_of(f, l):
        return jnp.broadcast_to(block(f, l)[:, 0:1], (sblk, nz))

    def take_off(f, l, full):
        xs = slice(1 + l * per, 1 + (l + 1) * per)
        f[last, xs, YB : YB + cy, :] = (block(f, l) - jnp.where(first_lane, full, 0.0)).reshape(per, cy, nz)

    def part(delta, size, base_at, src_base):
        if delta == 0:
            return pl.ds(src_base, size), pl.ds(base_at, size)
        if delta < 0:
            return pl.ds(src_base, 1), pl.ds(base_at + size, 1)
        return pl.ds(src_base + size - 1, 1), pl.ds(base_at - 1, 1)

    def halo_send(f, at, size, send_sem, recv_sem):
        cs = pl.ds(at, size)
        for dx, dy in DIRS:
            @pl.when(exists(dx, dy))
            def _():
                sx, tx = part(dx, cx, 1, 1)
                sy, ty = part(dy, cy, YB, YB)
                pltpu.make_async_remote_copy(
                    src_ref=f.at[cs, sx, sy], dst_ref=f.at[cs, tx, ty], send_sem=send_sem, recv_sem=recv_sem,
                    device_id={"gx": gx + dx, "gy": gy + dy}, device_id_type=MESH).start()

    def halo_send_args():
        for dx, dy in DIRS:
            @pl.when(exists(dx, dy))
            def _():
                sx, tx = part(dx, cx, 1, 0)
                sy, ty = part(dy, cy, YB, 0)
                for src, dst in ((disp.at[0, :, sx, sy], f0.at[pl.ds(0, comp), tx, ty]),
                                 (kappa.at[:, sx, sy], f0.at[pl.ds(comp, 1), tx, ty])):
                    pltpu.make_async_remote_copy(
                        src_ref=src, dst_ref=dst, send_sem=hs.at[0], recv_sem=hr.at[0],
                        device_id={"gx": gx + dx, "gy": gy + dy}, device_id_type=MESH).start()

    def surf_send(r):
        for k in reversed(range(ngx)):
            pltpu.make_async_remote_copy(
                src_ref=s1b.at[r, gx], dst_ref=s1b.at[r, gx], send_sem=ss.at[0], recv_sem=sr.at[r],
                device_id={"body": 0, "gx": far(gx, k, ngx)}, device_id_type=MESH).start()

    def surface_rows(f, r):
        for l in range(bpd):
            s1b[r, gx, l] = to_row(first_of(f, l))

    def pulled_send(first, size, recv_sem):
        ks = pl.ds(first, size)

        def go(bo, g):
            pltpu.make_async_remote_copy(
                src_ref=pbuf.at[1, gx, ks], dst_ref=pbuf.at[1, gx, ks], send_sem=ps.at[0], recv_sem=recv_sem,
                device_id={"body": bo, "gx": g}, device_id_type=MESH).start()
        for k in reversed(range(ngx)):
            go(1, far(gx, k, ngx))
            if k:
                go(0, far(gx, k, ngx))

    def pass_on(r, first, size):
        ks = pl.ds(first, size)
        for s in (-1, 1):
            @pl.when(exists(0, s))
            def _():
                pltpu.make_async_remote_copy(
                    src_ref=pbuf.at[1, :, ks], dst_ref=pbuf.at[1 - s, :, ks], send_sem=ps.at[0],
                    recv_sem=pn.at[r, (1 - s) // 2], device_id={"gy": gy + s}, device_id_type=MESH).start()

    def expand(d, k):
        u = jnp.zeros((rowblk, sblk), f32)
        for g in range(ngx):
            for l in range(bpd):
                u = u + jnp.where(block_f == pbuf[d, g, 1, l], pbuf[d, g, k, l], 0.0)
        return u

    def ring_fix(f, r, k, size):
        wait_rows(pr.at[r], ngx * size * bpd)
        pass_on(r, k, size)
        ub[1, 1 : 1 + rowblk] = expand(1, k).reshape(rowblk, 1, sblk)

        def row(d, j):
            return ub[d, gx * bpd + j]

        for l in range(bpd):
            take_off(f, l, to_full(row(1, 1 + l)))
        for j, x, at in ((0, 0, sblk - cy), (bpd + 1, cx + 1, 0)):
            col = jnp.sum(jnp.where(eye[at : at + cy], row(1, j), 0.0), axis=1, keepdims=True)
            f[last, x, YB : YB + cy, :] = f[last, x, YB : YB + cy, :] - jnp.where(lane_row == 0, col, 0.0)
        for d, y, off in ((0, YB - 1, cy - 1), (2, YB + cy, 0)):
            pl.when(exists(0, d - 1))(lambda: wait_rows(pn.at[r, d // 2], ngx * size * bpd))
            ub[d, 1 : 1 + rowblk] = expand(d, k).reshape(rowblk, 1, sblk)
            for xi in range(cx + 2):
                j = (xi - 1 + per) // per
                at = ((xi - 1 + per) % per) * cy + off
                val = pltpu.roll(row(d, j), (nz - at) % nz, 1)
                f[last, xi, y : y + 1, :] = f[last, xi, y : y + 1, :] - jnp.where(lane_one == 0, val, 0.0)

    def apply(f, c, emit):
        window = []
        for x in range(cx + 2):
            kap = [f0[comp, x, YB + s : YB + s + cy, :] for s in (-1, 0, 1)]
            val = [f[c, x, YB + s : YB + s + cy, :] for s in (-1, 0, 1)]
            window.append((val[1] + 0.5 * (val[0] + val[2]),
                           kap[1] * val[1] + 0.5 * (kap[0] * val[0] + kap[2] * val[2])))
            if x >= 2:
                p = window[x - 1][0] + 0.5 * (window[x - 2][0] + window[x][0])
                q = window[x - 1][1] + 0.5 * (window[x - 2][1] + window[x][1])
                k0 = f0[comp, x - 1, YB : YB + cy, :]
                v0 = f[c, x - 1, YB : YB + cy, :]
                emit(c, x - 2, diag[x - 2] * v0 - k0 * tz(p) - tz(q))

    def make_diag():
        window = []
        for x in range(cx + 2):
            kap = [f0[comp, x, YB + s : YB + s + cy, :] for s in (-1, 0, 1)]
            window.append(kap[1] + 0.5 * (kap[0] + kap[2]))
            if x >= 2:
                p = window[x - 1] + 0.5 * (window[x - 2] + window[x])
                diag[x - 2] = sigma_v[x - 2] + 8.0 * f0[comp, x - 1, YB : YB + cy, :] + tz(p)

    def emit_rhs(c, x, val):
        f1[c, 1 + x, YB : YB + cy, :] = force_v[c, x] - val

    def emit_v1(c, x, val):
        f2[c, 1 + x, YB : YB + cy, :] = val

    def r0_of(c, x):
        return f1[c, 1 + x, YB : YB + cy, :]

    def v1_of(c, x):
        return f2[c, 1 + x, YB : YB + cy, :]

    def fold(v):
        return jnp.sum(v.reshape(cy // 8, 8, nz), axis=0)

    def gather(c, wanted, fields):
        sums = {}
        for x in range(cx):
            for k, (left, right) in wanted.items():
                term = fold(fields(x)[left] * fields(x)[right])
                sums[k] = sums[k] + term if k in sums else term
        for k, v in sums.items():
            acc[k] = acc[k] + v

    def dots(c):
        gather(c, {RR: (0, 0), RV: (0, 1), VV: (1, 1)}, lambda x: (r0_of(c, x), v1_of(c, x)))

    def total(v):
        return jnp.sum(jnp.sum(v, axis=0, keepdims=True), axis=1, keepdims=True)

    def choose_own():
        rv, vv = total(acc[RV]), total(acc[VV])
        own = jnp.where(vv > 0.0, rv / jnp.where(vv > 0.0, vv, 1.0), 0.0)
        own_ref[...] = jnp.broadcast_to(own, (cy, nz))

    def near_dots(c):
        own = own_ref[...]
        gather(c, {NN: (0, 0), NV: (0, 1)}, lambda x: (r0_of(c, x) - own * v1_of(c, x), v1_of(c, x)))

    def image_dots(c, more):
        own = own_ref[...]
        sums = {}

        def emit(c, x, val):
            v = v1_of(c, x)
            r = r0_of(c, x)
            near = r - own * v
            terms = {NW: near * val, VW: v * val}
            if more:
                terms.update({RV: r * v, VV: v * v, NN: near * near, NV: near * v})
            for k, t in terms.items():
                sums[k] = sums[k] + fold(t) if k in sums else fold(t)
        apply(f2, c, emit)
        for k, v in sums.items():
            acc[k] = acc[k] + v

    def first_comps(act):
        @pl.loop(0, last)
        def _(c):
            act(c)

    def gap_of(l, s1):
        picked = jnp.sum(jnp.where(block_of == partner[l], s1, 0.0), axis=0, keepdims=True)
        return base[l] - jnp.broadcast_to(jnp.sum(mort[l] * picked, axis=1, keepdims=True), (sblk, nz))

    def pull(l, k, t):
        pbuf[1, gx, k, l] = jnp.sum(mort[l] * t, axis=0, keepdims=True)

    def surf_rows(r):
        return s1b[r].reshape(rowblk, sblk)

    def send_final():
        sub = lax.broadcasted_iota(jnp.int32, (8, nz), 0)
        stack = jnp.zeros((8, nz), f32)
        for k in range(OWN):
            stack = jnp.where(sub == k, jnp.broadcast_to(jnp.sum(acc[k], axis=0, keepdims=True), (8, nz)), stack)
        lanes = lax.broadcasted_iota(jnp.int32, (8, nz), 1)
        stack = jnp.where((sub == OWN) & (lanes == 0), own_ref[0:8, :], stack)
        final[me] = jnp.sum(jnp.where(sub == lanes, jnp.sum(stack, axis=1, keepdims=True), 0.0), axis=0, keepdims=True)

        def go(place):
            pltpu.make_async_remote_copy(
                src_ref=final.at[me], dst_ref=final.at[me], send_sem=fin.at[0], recv_sem=fin.at[1],
                device_id=place, device_id_type=MESH).start()
        if count <= 64:
            for kx in reversed(range(ngx)):
                for ky in reversed(range(ngy)):
                    for kb in reversed(range(nb)):
                        if kx or ky or kb:
                            go({"body": far(b, kb, nb), "gx": far(gx, kx, ngx), "gy": far(gy, ky, ngy)})
        else:
            each_peer(lambda k: go(place_of(lax.rem(me + k, count))))

    pl.semaphore_wait(barrier, expect)

    @pl.when(b == 1)
    def _():
        wait_rows(ls.at[0], cx * cy)
        surface_rows(f0, 0)
        surf_send(0)

    halo_send_args()

    @pl.when(b == 1)
    def _():
        wait_rows(ls.at[1], comp * cx * cy)
        wait_rows(ls.at[2], (comp + 1) * cx * cy)
        wait_halo(hr.at[0], comp + 1)
        make_diag()
        apply(f0, last, emit_rhs)
        surface_rows(f1, 1)
        surf_send(1)
        halo_send(f1, last, 1, hs.at[1], hr.at[2])
        first_comps(lambda c: apply(f0, c, emit_rhs))
        halo_send(f1, 0, last, hs.at[0], hr.at[1])

        wait_halo(hr.at[1], last)
        first_comps(lambda c: apply(f1, c, emit_v1))
        halo_send(f2, 0, last, hs.at[0], hr.at[3])
        first_comps(dots)
        choose_own()
        first_comps(near_dots)
        wait_halo(hs.at[1], 1)
        wait_halo(hr.at[2], 1)
        ring_fix(f1, 0, 0, 2)
        apply(f1, last, emit_v1)
        surface_rows(f2, 2)
        surf_send(2)
        halo_send(f2, last, 1, hs.at[2], hr.at[4])
        gather(last, {RR: (0, 0)}, lambda x: (r0_of(last, x),))

        wait_halo(hr.at[3], last)
        first_comps(lambda c: image_dots(c, False))
        wait_halo(hs.at[2], 1)
        wait_halo(hr.at[4], 1)
        ring_fix(f2, 1, 2, 1)
        image_dots(last, True)
        send_final()

    @pl.when(b == 0)
    def _():
        for k in range(4):
            sem, rows = ((ls.at[0], cx * cy), (ls.at[3], 2 * bpd), (ls.at[6], bpd * sblk), (ls.at[1], comp * cx * cy))[k]
            wait_rows(sem, rows)
        pltpu.make_async_copy(partner_in, partner, ls.at[4]).wait()
        pltpu.make_async_copy(active_in, active, ls.at[5]).wait()
        for l in range(bpd):
            base[l] = to_full(gap0[l : l + 1, :]) - first_of(f0, l)
            prs_f[l] = to_full(press[l : l + 1, :])
            pbuf[1, gx, 1, l] = jnp.full((1, sblk), partner[l].astype(f32))
        wait_rows(sr.at[0], ngx * bpd)
        s1 = surf_rows(0)
        for l in range(bpd):
            gap = gap_of(l, s1)
            prs = prs_f[l]
            radius = jnp.sqrt(gap * gap + prs * prs + 0.01)
            per_radius = 1.0 / radius
            per_divisor = 1.0 / ((1.0 - prs * per_radius) + 0.5)
            flag = active[l].astype(f32)
            excess = (gap + prs - radius) * per_divisor
            slope = (1.0 - gap * per_radius) * per_divisor
            t = flag * (prs - excess)
            pull(l, 0, t)
            t_f[l] = t
            ex_f[l] = excess
            sl_f[l] = slope
            st_f[l] = flag * slope
        pulled_send(0, 2, pr.at[0])
        wait_rows(ls.at[2], (comp + 1) * cx * cy)
        wait_halo(hr.at[0], comp + 1)
        make_diag()
        first_comps(lambda c: apply(f0, c, emit_rhs))
        halo_send(f1, 0, last, hs.at[0], hr.at[1])
        apply(f0, last, emit_rhs)
        for l in range(bpd):
            take_off(f1, l, t_f[l])
        halo_send(f1, last, 1, hs.at[1], hr.at[2])
        for l in range(bpd):
            base[l] = -first_of(f1, l)

        wait_rows(sr.at[1], ngx * bpd)
        if ngx > 1:
            wait_rows(pr.at[0], (ngx - 1) * 2 * bpd)
        s1 = surf_rows(1) - expand(1, 0)
        for l in range(bpd):
            gap = gap_of(l, s1)
            t = st_f[l] * gap
            pull(l, 2, t)
            t_f[l] = t
            gr_f[l] = gap
        pulled_send(2, 1, pr.at[1])
        wait_halo(hr.at[1], last)
        first_comps(lambda c: apply(f1, c, emit_v1))
        halo_send(f2, 0, last, hs.at[0], hr.at[3])
        wait_halo(hr.at[2], 1)
        apply(f1, last, emit_v1)
        for l in range(bpd):
            take_off(f2, l, t_f[l])
        halo_send(f2, last, 1, hs.at[2], hr.at[4])
        for l in range(bpd):
            base[l] = -first_of(f2, l)
        first_comps(dots)
        choose_own()
        dots(last)
        pl.loop(0, comp)(near_dots)
        wait_halo(hr.at[3], last)
        wait_halo(hr.at[4], 1)
        pl.loop(0, comp)(lambda c: image_dots(c, False))

        wait_rows(sr.at[2], ngx * bpd)
        if ngx > 1:
            wait_rows(pr.at[1], (ngx - 1) * bpd)
        s1 = surf_rows(2) - expand(1, 2)
        own = own_ref[0:1, :]
        for l in range(bpd):
            gap = gap_of(l, s1)
            gv_f[l] = gap
            weighted = st_f[l] * gap
            for k, left in ((NW, gr_f[l] - own * gap), (VW, gap)):
                row = jnp.sum(weighted * left, axis=0, keepdims=True)
                acc[k, 0:1] = acc[k, 0:1] + jnp.where(lane_one == 0, row, 0.0)
        send_final()
        for l in range(bpd):
            flag = active[l].astype(f32)
            npr[0, l] = flag * (press[l : l + 1, :] - to_row(ex_f[l]))
            npr[1, l] = flag * to_row(sl_f[l] * gr_f[l])
            npr[2, l] = flag * to_row(sl_f[l] * gv_f[l])
        pltpu.make_async_remote_copy(src_ref=npr, dst_ref=npr, send_sem=nps.at[0], recv_sem=nps.at[1],
                                     device_id={"body": 1}, device_id_type=MESH).start()

    @pl.when(b == 1)
    def _():
        wait_rows(ls.at[3], 2 * bpd)
        wait_rows(ls.at[6], bpd * sblk)
        pltpu.make_async_copy(partner_in, partner, ls.at[4]).wait()
        pltpu.make_async_copy(active_in, active, ls.at[5]).wait()
        wait_rows(ss.at[0], 3 * ngx * bpd)
        for c in sides(ngy):
            if c:
                pl.when(nys == c)(lambda: wait_rows(ps.at[0], 3 * bpd * c * ngx))
        wait_rows(nps.at[1], 3 * bpd)

    @pl.when(b == 0)
    def _():
        wait_rows(ps.at[0], 3 * bpd * (2 * ngx - 1))
        wait_halo(hs.at[1], 1)
        wait_halo(hs.at[2], 1)
        wait_rows(nps.at[0], 3 * bpd)

    wait_halo(hs.at[0], comp + 1 + 2 * last)
    wait_rows(fin.at[0], count - 1)
    for c in range(comp):
        for x in range(cx):
            r0_out[c, x] = r0_of(c, x)
            v1_out[c, x] = v1_of(c, x)
    npr_out[...] = npr[...]

    wait_rows(fin.at[1], count - 1)
    table = final[...].reshape(count, sblk)
    lanes = lax.broadcasted_iota(jnp.int32, (count, sblk), 1)
    sums = jnp.sum(table, axis=0, keepdims=True)
    norm0 = sums[:, RR : RR + 1]
    alpha0 = norm0 / sums[:, RV : RV + 1]
    delta = alpha0 - table[:, OWN : OWN + 1]

    def pick(weights):
        w = jnp.zeros((count, sblk), f32)
        for k, v in weights:
            w = jnp.where(lanes == k, v, w)
        return total(w * table)

    norm1 = pick(((NN, 1.0), (NV, -2.0 * delta), (VV, delta * delta)))
    product1 = pick(((NV, 1.0), (VV, -delta), (NW, -alpha0), (VW, alpha0 * delta)))
    ratio = norm1 / norm0
    alpha1 = norm1 / (product1 - ratio * norm1 / alpha0)
    coef[0:1, :] = jnp.broadcast_to(alpha0 + alpha1 * (1.0 + ratio), (1, nz))
    coef[1:2, :] = jnp.broadcast_to(-alpha1 * alpha0, (1, nz))


def out_kernel(r0, v1, coef, npr, inc, new_press, buf, rows, sems):
    comp, cx, cy, nz = buf.shape
    bpd = rows.shape[0]
    cr, cv = coef[0:1, :], coef[1:2, :]
    copies = []
    for c in range(comp):
        for x in range(cx):
            buf[c, x] = cr * r0[c, x] + cv * v1[c, x]
        copies.append(pltpu.make_async_copy(buf.at[c], inc.at[0, c], sems.at[c]))
        copies[-1].start()
    for l in range(bpd):
        rows[l : l + 1, :] = npr[0, l] - (cr * npr[1, l] + cv * npr[2, l])
    copies.append(pltpu.make_async_copy(rows, new_press, sems.at[comp]))
    copies[-1].start()
    for copy in copies:
        copy.wait()


def on_device(disp, force, kappa, sigma, gap0, pressure, mortar, partner, active):
    nb, ngx, ngy = (lax.axis_size(a) for a in ("body", "gx", "gy"))
    _, comp, cx, cy, nz = disp.shape
    bpd, sblk, _ = mortar.shape
    f32 = jnp.float32
    any_spec = pl.BlockSpec(memory_space=pl.ANY)
    vmem = pl.BlockSpec(memory_space=pltpu.VMEM)
    rows = cy + 2 * YB
    rowblk = ngx * bpd
    count = nb * ngx * ngy
    dma = pltpu.SemaphoreType.DMA
    full = pltpu.VMEM((bpd, sblk, nz), f32)
    most = max((comp + 1) * cx * cy, (comp + 1 + 2 * (comp - 1)) * 2 * (cy + cx + 2), count, bpd * sblk,
               3 * bpd * 4 * ngx)
    field = (comp, cx + 2, rows, nz)
    r0, v1, coef, npr = pl.pallas_call(
        functools.partial(kernel, nb, ngx, ngy),
        out_shape=(pltpu.VMEM((comp, cx, cy, nz), f32), pltpu.VMEM((comp, cx, cy, nz), f32), pltpu.VMEM((8, nz), f32),
                   pltpu.VMEM((3, bpd, 1, sblk), f32)),
        in_specs=[any_spec] * 9,
        out_specs=(vmem,) * 4,
        scratch_shapes=[
            pltpu.VMEM((bpd, sblk), f32),
            pltpu.VMEM((bpd, sblk), f32),
            pltpu.SMEM((bpd,), jnp.int32),
            pltpu.SMEM((bpd,), jnp.int32),
            pltpu.VMEM((comp + 1, cx + 2, rows, nz), f32),
            pltpu.VMEM(field, f32),
            pltpu.VMEM(field, f32),
            pltpu.VMEM((3, bpd, 1, sblk), f32),
            pltpu.VMEM((cx, cy, nz), f32),
            pltpu.VMEM((comp, cx, cy, nz), f32),
            pltpu.VMEM((cx, cy, nz), f32),
            pltpu.VMEM((bpd, sblk, sblk), f32),
            pltpu.VMEM((3, ngx, bpd, 1, sblk), f32),
            pltpu.VMEM((3, ngx, 3, bpd, 1, sblk), f32),
            pltpu.VMEM((3, rowblk + 2, 1, sblk), f32),
            full, full, full, full, full, full, full, full,
            pltpu.VMEM((8, 8, nz), f32),
            pltpu.VMEM((cy, nz), f32),
            pltpu.VMEM((count, 1, sblk), f32),
            pltpu.VMEM((most, 1, nz), f32),
            dma((7,)), dma((5,)), dma((3,)), dma((3,)), dma((1,)), dma((2,)), dma((2, 2)), dma((1,)), dma((2,)),
            dma((2,)),
        ],
        compiler_params=pltpu.CompilerParams(collective_id=0, has_side_effects=True,
                                             vmem_limit_bytes=60 * 1024 * 1024),
        name="newton_step",
    )(disp, force, kappa, sigma, gap0, pressure, mortar, partner, active)
    return pl.pallas_call(
        out_kernel,
        out_shape=(jax.ShapeDtypeStruct(disp.shape, f32), jax.ShapeDtypeStruct(gap0.shape, f32)),
        in_specs=[vmem] * 4,
        out_specs=(any_spec, any_spec),
        scratch_shapes=[pltpu.VMEM((comp, cx, cy, nz), f32), pltpu.VMEM((bpd, sblk), f32), dma((comp + 1,))],
        compiler_params=pltpu.CompilerParams(vmem_limit_bytes=4 * 1024 * 1024),
        name="newton_out",
    )(r0, v1, coef, npr)


def solution(mesh):
    placed = (
        P("body", None, "gx", "gy", None),
        P("body", None, "gx", "gy", None),
        P("body", "gx", "gy", None),
        P("body", "gx", "gy", None),
        P(("gx", "gy"), None),
        P(("gx", "gy"), None),
        P(("gx", "gy"), None, None),
        P(("gx", "gy")),
        P(("gx", "gy")),
    )
    return jax.shard_map(
        on_device,
        mesh=mesh,
        in_specs=placed,
        out_specs=(P("body", None, "gx", "gy", None), P(("gx", "gy"), None)),
        check_vma=False,
    )
```

time: 30.3 us -> 27.3 us (0.901)
  Pallas kernels: 28.2 us -> 26.5 us
  local copies, waits for them, and re-layouts: 1.31 us -> 0 us
    pallas_call x1, Pallas kernels: 28.2 us -> 25.7 us  [on_device(): pl.pallas_call(functools.partial(kernel, nb, ngx, ngy), out_shape=(pltpu....]
    unnamed x2 -> x0, local copies, waits for them, and re-layouts: 1.31 us -> none
    pallas_call x0 -> x1, Pallas kernels: none -> 0.8 us  [on_device(): pl.pallas_call(out_kernel, out_shape=(jax.ShapeDtypeStruct(disp.shape, f3...]
where the time goes in v1:
time: 27.3 us; the launch traced here: 27.2 us
  Pallas kernels  26.5 us (97%)
  between operations  0.64 us (2%)
    pallas_call x1, Pallas kernels, on_device(): pl.pallas_call(functools.partial(kernel, nb, ngx, ngy), out_shape=(pltpu....  25.7 us
    pallas_call x1, Pallas kernels, on_device(): pl.pallas_call(out_kernel, out_shape=(jax.ShapeDtypeStruct(disp.shape, f3...  0.8 us

profile of v1, /device:TPU:0, one launch (start us, length us, event | category | flops | bytes accessed | tf_op | source)
XLA Modules:
  0.0 27.2 jit_solution(15956225037667007930)
XLA Ops:
  0.6 25.7 %newton_step.1 = (f32[3,8,32,128]{3,2,1,0:T(8,128)S(1)}, f32[3,8,32,128]{3,2,1,0:T(8,128)S(1)}, f32[8,128]{1,0:T(8,128)S(1)}, f32[3,2,1,128]{3,2,1,0:T(1,128)S(1)}) custom-call(f32[1,3,8,32,128]{4,3,2,1,0:T(8,128)} %disp.1, f32[1,3,8,32,128]{4,3,2,1,0:T(8,128)} %force.1, f32[1,8,32,128]{3,2,1,0:T(8,128)} %kappa.1, f32[1,8,32,128]{3,2,1,0:T(8,128)} %sigma.1, ...), custom_call_target="tpu_custom_call" | custom-call | tf_op jit(solution)/shard_map/newton_step/pallas_call | solution.py:594
  26.4 0.8 %newton_out.1 = (f32[1,3,8,32,128]{4,3,2,1,0:T(8,128)}, f32[2,128]{1,0:T(2,128)}) custom-call(f32[3,8,32,128]{3,2,1,0:T(8,128)S(1)} %get-tuple-element.6.r0, f32[3,8,32,128]{3,2,1,0:T(8,128)S(1)} %get-tuple-element.7.v1, f32[8,128]{1,0:T(8,128)S(1)} %get-tuple-element.8.coef, f32[3,2,1,128]{3,2,1,0:T(1,128)S(1)} %get-tuple-element.9.npr), custom_call_target="tpu_custom_call" | custom-call | tf_op jit(solution)/shard_map/newton_out/pallas_call | solution.py:628

commit v2 on v1

--- a/solution.py
+++ b/solution.py
@@ -18,7 +18,7 @@
            r0_out, v1_out, coef, npr_out,
            gap0, press, partner, active, f0, f1, f2, npr, diag, force_v, sigma_v, mort, s1b, pbuf, ub, base, prs_f, t_f, ex_f, sl_f,
            st_f, gr_f, gv_f, acc, own_ref, final, dummy,
-           ls, hr, hs, sr, ss, pr, pn, ps, nps, fin):
+           ls, hr, hs, sr, ss, pr, pq, pn, ps, nps, fin):
     comp, cx, cy, nz = force_v.shape
     bpd, sblk = gap0.shape
     per = sblk // cy
@@ -206,26 +206,29 @@
         for l in range(bpd):
             s1b[r, gx, l] = to_row(first_of(f, l))
 
-    def pulled_send(first, size, recv_sem):
+    def pulled_send(first, size, r):
         ks = pl.ds(first, size)
 
-        def go(bo, g):
+        def go(bo, g, sem):
             pltpu.make_async_remote_copy(
-                src_ref=pbuf.at[1, gx, ks], dst_ref=pbuf.at[1, gx, ks], send_sem=ps.at[0], recv_sem=recv_sem,
+                src_ref=pbuf.at[1, gx, ks], dst_ref=pbuf.at[1, gx, ks], send_sem=ps.at[0], recv_sem=sem,
                 device_id={"body": bo, "gx": g}, device_id_type=MESH).start()
-        for k in reversed(range(ngx)):
-            go(1, far(gx, k, ngx))
-            if k:
-                go(0, far(gx, k, ngx))
+        go(1, gx, pq.at[r])
+        for k in reversed(range(1, ngx)):
+            go(1, far(gx, k, ngx), pr.at[r])
+            go(0, far(gx, k, ngx), pr.at[r])
 
     def pass_on(r, first, size):
         ks = pl.ds(first, size)
+        wait_rows(pq.at[r], size * bpd)
         for s in (-1, 1):
             @pl.when(exists(0, s))
             def _():
-                pltpu.make_async_remote_copy(
-                    src_ref=pbuf.at[1, :, ks], dst_ref=pbuf.at[1 - s, :, ks], send_sem=ps.at[0],
-                    recv_sem=pn.at[r, (1 - s) // 2], device_id={"gy": gy + s}, device_id_type=MESH).start()
+                for k in reversed(range(ngx)):
+                    pltpu.make_async_remote_copy(
+                        src_ref=pbuf.at[1, gx, ks], dst_ref=pbuf.at[1 - s, gx, ks], send_sem=ps.at[0],
+                        recv_sem=pn.at[r, (1 - s) // 2], device_id={"gx": far(gx, k, ngx), "gy": gy + s},
+                        device_id_type=MESH).start()
 
     def expand(d, k):
         u = jnp.zeros((rowblk, sblk), f32)
@@ -235,8 +238,8 @@
         return u
 
     def ring_fix(f, r, k, size):
-        wait_rows(pr.at[r], ngx * size * bpd)
-        pass_on(r, k, size)
+        if ngx > 1:
+            wait_rows(pr.at[r], (ngx - 1) * size * bpd)
         ub[1, 1 : 1 + rowblk] = expand(1, k).reshape(rowblk, 1, sblk)
 
         def row(d, j):
@@ -247,6 +250,8 @@
         for j, x, at in ((0, 0, sblk - cy), (bpd + 1, cx + 1, 0)):
             col = jnp.sum(jnp.where(eye[at : at + cy], row(1, j), 0.0), axis=1, keepdims=True)
             f[last, x, YB : YB + cy, :] = f[last, x, YB : YB + cy, :] - jnp.where(lane_row == 0, col, 0.0)
+        if r == 0:
+            pass_on(1, 2, 1)
         for d, y, off in ((0, YB - 1, cy - 1), (2, YB + cy, 0)):
             pl.when(exists(0, d - 1))(lambda: wait_rows(pn.at[r, d // 2], ngx * size * bpd))
             ub[d, 1 : 1 + rowblk] = expand(d, k).reshape(rowblk, 1, sblk)
@@ -392,6 +397,7 @@
         surface_rows(f1, 1)
         surf_send(1)
         halo_send(f1, last, 1, hs.at[1], hr.at[2])
+        pass_on(0, 0, 2)
         first_comps(lambda c: apply(f0, c, emit_rhs))
         halo_send(f1, 0, last, hs.at[0], hr.at[1])
 
@@ -446,7 +452,7 @@
             ex_f[l] = excess
             sl_f[l] = slope
             st_f[l] = flag * slope
-        pulled_send(0, 2, pr.at[0])
+        pulled_send(0, 2, 0)
         wait_rows(ls.at[2], (comp + 1) * cx * cy)
         wait_halo(hr.at[0], comp + 1)
         make_diag()
@@ -469,7 +475,7 @@
             pull(l, 2, t)
             t_f[l] = t
             gr_f[l] = gap
-        pulled_send(2, 1, pr.at[1])
+        pulled_send(2, 1, 1)
         wait_halo(hr.at[1], last)
         first_comps(lambda c: apply(f1, c, emit_v1))
         halo_send(f2, 0, last, hs.at[0], hr.at[3])
@@ -618,7 +624,7 @@
             pltpu.VMEM((cy, nz), f32),
             pltpu.VMEM((count, 1, sblk), f32),
             pltpu.VMEM((most, 1, nz), f32),
-            dma((7,)), dma((5,)), dma((3,)), dma((3,)), dma((1,)), dma((2,)), dma((2, 2)), dma((1,)), dma((2,)),
+            dma((7,)), dma((5,)), dma((3,)), dma((3,)), dma((1,)), dma((2,)), dma((2,)), dma((2, 2)), dma((1,)), dma((2,)),
             dma((2,)),
         ],
         compiler_params=pltpu.CompilerParams(collective_id=0, has_side_effects=True,

time: 27.3 us -> 25.2 us (0.923)
  Pallas kernels: 26.5 us -> 24.4 us
    pallas_call x1, Pallas kernels: 25.7 us -> 23.6 us  [on_device(): pl.pallas_call(functools.partial(kernel, nb, ngx, ngy), out_shape=(pltpu....]
where the time goes in v2:
time: 25.2 us; the launch traced here: 25.1 us
  Pallas kernels  24.4 us (97%)
  between operations  0.64 us (3%)
    pallas_call x1, Pallas kernels, on_device(): pl.pallas_call(functools.partial(kernel, nb, ngx, ngy), out_shape=(pltpu....  23.6 us
    pallas_call x1, Pallas kernels, on_device(): pl.pallas_call(out_kernel, out_shape=(jax.ShapeDtypeStruct(disp.shape, f3...  0.8 us

profile of v2, /device:TPU:0, one launch (start us, length us, event | category | flops | bytes accessed | tf_op | source)
XLA Modules:
  0.0 25.1 jit_solution(16584481335405357567)
XLA Ops:
  0.6 23.6 %newton_step.1 = (f32[3,8,32,128]{3,2,1,0:T(8,128)S(1)}, f32[3,8,32,128]{3,2,1,0:T(8,128)S(1)}, f32[8,128]{1,0:T(8,128)S(1)}, f32[3,2,1,128]{3,2,1,0:T(1,128)S(1)}) custom-call(f32[1,3,8,32,128]{4,3,2,1,0:T(8,128)} %disp.1, f32[1,3,8,32,128]{4,3,2,1,0:T(8,128)} %force.1, f32[1,8,32,128]{3,2,1,0:T(8,128)} %kappa.1, f32[1,8,32,128]{3,2,1,0:T(8,128)} %sigma.1, ...), custom_call_target="tpu_custom_call" | custom-call | tf_op jit(solution)/shard_map/newton_step/pallas_call | solution.py:600
  24.3 0.8 %newton_out.1 = (f32[1,3,8,32,128]{4,3,2,1,0:T(8,128)}, f32[2,128]{1,0:T(2,128)}) custom-call(f32[3,8,32,128]{3,2,1,0:T(8,128)S(1)} %get-tuple-element.6.r0, f32[3,8,32,128]{3,2,1,0:T(8,128)S(1)} %get-tuple-element.7.v1, f32[8,128]{1,0:T(8,128)S(1)} %get-tuple-element.8.coef, f32[3,2,1,128]{3,2,1,0:T(1,128)S(1)} %get-tuple-element.9.npr), custom_call_target="tpu_custom_call" | custom-call | tf_op jit(solution)/shard_map/newton_out/pallas_call | solution.py:634

commit v3 on v2

--- a/solution.py
+++ b/solution.py
@@ -10,7 +10,10 @@
 MESH = pl.DeviceIdType.MESH
 YB = 8
 CORNERS = tuple((dx, dy) for dx in (-1, 1) for dy in (-1, 1))
-DIRS = CORNERS + ((0, -1), (0, 1), (-1, 0), (1, 0))
+ALONG_Y = ((0, -1), (0, 1))
+ACROSS_X = CORNERS + ((-1, 0), (1, 0))
+FACES_X = ((-1, 0), (1, 0))
+DIRS = CORNERS + ALONG_Y + FACES_X
 RR, RV, VV, NN, NV, NW, VW, OWN = range(8)
 
 
@@ -173,9 +176,9 @@
             return pl.ds(src_base, 1), pl.ds(base_at + size, 1)
         return pl.ds(src_base + size - 1, 1), pl.ds(base_at - 1, 1)
 
-    def halo_send(f, at, size, send_sem, recv_sem):
+    def halo_send(f, at, size, send_sem, recv_sem, dirs):
         cs = pl.ds(at, size)
-        for dx, dy in DIRS:
+        for dx, dy in dirs:
             @pl.when(exists(dx, dy))
             def _():
                 sx, tx = part(dx, cx, 1, 1)
@@ -184,8 +187,8 @@
                     src_ref=f.at[cs, sx, sy], dst_ref=f.at[cs, tx, ty], send_sem=send_sem, recv_sem=recv_sem,
                     device_id={"gx": gx + dx, "gy": gy + dy}, device_id_type=MESH).start()
 
-    def halo_send_args():
-        for dx, dy in DIRS:
+    def halo_send_args(dirs):
+        for dx, dy in dirs:
             @pl.when(exists(dx, dy))
             def _():
                 sx, tx = part(dx, cx, 1, 0)
@@ -261,19 +264,29 @@
                 val = pltpu.roll(row(d, j), (nz - at) % nz, 1)
                 f[last, xi, y : y + 1, :] = f[last, xi, y : y + 1, :] - jnp.where(lane_one == 0, val, 0.0)
 
-    def apply(f, c, emit):
+    def planes(f, c, emit, first, stop):
         window = []
-        for x in range(cx + 2):
+        for x in range(first, stop + 2):
             kap = [f0[comp, x, YB + s : YB + s + cy, :] for s in (-1, 0, 1)]
             val = [f[c, x, YB + s : YB + s + cy, :] for s in (-1, 0, 1)]
             window.append((val[1] + 0.5 * (val[0] + val[2]),
                            kap[1] * val[1] + 0.5 * (kap[0] * val[0] + kap[2] * val[2])))
-            if x >= 2:
-                p = window[x - 1][0] + 0.5 * (window[x - 2][0] + window[x][0])
-                q = window[x - 1][1] + 0.5 * (window[x - 2][1] + window[x][1])
+            if len(window) >= 3:
+                p = window[-2][0] + 0.5 * (window[-3][0] + window[-1][0])
+                q = window[-2][1] + 0.5 * (window[-3][1] + window[-1][1])
                 k0 = f0[comp, x - 1, YB : YB + cy, :]
                 v0 = f[c, x - 1, YB : YB + cy, :]
                 emit(c, x - 2, diag[x - 2] * v0 - k0 * tz(p) - tz(q))
+
+    def apply(f, c, emit):
+        planes(f, c, emit, 0, cx)
+
+    def edges(f, c, emit):
+        planes(f, c, emit, 0, 1)
+        planes(f, c, emit, cx - 1, cx)
+
+    def inside(f, c, emit):
+        planes(f, c, emit, 1, cx - 1)
 
     def make_diag():
         window = []
@@ -289,6 +302,16 @@
 
     def emit_v1(c, x, val):
         f2[c, 1 + x, YB : YB + cy, :] = val
+
+    def traction(x):
+        rows = slice((x % per) * cy, (x % per + 1) * cy)
+        return jnp.where(lane_row == 0, t_f[x // per, rows, :], 0.0)
+
+    def emit_rhs_t(c, x, val):
+        f1[c, 1 + x, YB : YB + cy, :] = force_v[c, x] - val - traction(x)
+
+    def emit_v1_t(c, x, val):
+        f2[c, 1 + x, YB : YB + cy, :] = val - traction(x)
 
     def r0_of(c, x):
         return f1[c, 1 + x, YB : YB + cy, :]
@@ -378,6 +401,7 @@
             each_peer(lambda k: go(place_of(lax.rem(me + k, count))))
 
     pl.semaphore_wait(barrier, expect)
+    halo_send_args(CORNERS + ALONG_Y)
 
     @pl.when(b == 1)
     def _():
@@ -385,7 +409,7 @@
         surface_rows(f0, 0)
         surf_send(0)
 
-    halo_send_args()
+    halo_send_args(FACES_X)
 
     @pl.when(b == 1)
     def _():
@@ -393,27 +417,35 @@
         wait_rows(ls.at[2], (comp + 1) * cx * cy)
         wait_halo(hr.at[0], comp + 1)
         make_diag()
-        apply(f0, last, emit_rhs)
+        first_comps(lambda c: edges(f0, c, emit_rhs))
+        halo_send(f1, 0, last, hs.at[0], hr.at[1], ACROSS_X)
+        edges(f0, last, emit_rhs)
+        halo_send(f1, last, 1, hs.at[1], hr.at[2], ACROSS_X)
+        inside(f0, last, emit_rhs)
         surface_rows(f1, 1)
         surf_send(1)
-        halo_send(f1, last, 1, hs.at[1], hr.at[2])
+        halo_send(f1, last, 1, hs.at[1], hr.at[2], ALONG_Y)
         pass_on(0, 0, 2)
-        first_comps(lambda c: apply(f0, c, emit_rhs))
-        halo_send(f1, 0, last, hs.at[0], hr.at[1])
+        first_comps(lambda c: inside(f0, c, emit_rhs))
+        halo_send(f1, 0, last, hs.at[0], hr.at[1], ALONG_Y)
 
         wait_halo(hr.at[1], last)
-        first_comps(lambda c: apply(f1, c, emit_v1))
-        halo_send(f2, 0, last, hs.at[0], hr.at[3])
+        first_comps(lambda c: edges(f1, c, emit_v1))
+        halo_send(f2, 0, last, hs.at[0], hr.at[3], ACROSS_X)
+        first_comps(lambda c: inside(f1, c, emit_v1))
+        halo_send(f2, 0, last, hs.at[0], hr.at[3], ALONG_Y)
+        wait_halo(hs.at[1], 1)
+        wait_halo(hr.at[2], 1)
+        ring_fix(f1, 0, 0, 2)
+        edges(f1, last, emit_v1)
+        halo_send(f2, last, 1, hs.at[2], hr.at[4], ACROSS_X)
+        inside(f1, last, emit_v1)
+        surface_rows(f2, 2)
+        surf_send(2)
+        halo_send(f2, last, 1, hs.at[2], hr.at[4], ALONG_Y)
         first_comps(dots)
         choose_own()
         first_comps(near_dots)
-        wait_halo(hs.at[1], 1)
-        wait_halo(hr.at[2], 1)
-        ring_fix(f1, 0, 0, 2)
-        apply(f1, last, emit_v1)
-        surface_rows(f2, 2)
-        surf_send(2)
-        halo_send(f2, last, 1, hs.at[2], hr.at[4])
         gather(last, {RR: (0, 0)}, lambda x: (r0_of(last, x),))
 
         wait_halo(hr.at[3], last)
@@ -456,12 +488,14 @@
         wait_rows(ls.at[2], (comp + 1) * cx * cy)
         wait_halo(hr.at[0], comp + 1)
         make_diag()
-        first_comps(lambda c: apply(f0, c, emit_rhs))
-        halo_send(f1, 0, last, hs.at[0], hr.at[1])
-        apply(f0, last, emit_rhs)
-        for l in range(bpd):
-            take_off(f1, l, t_f[l])
-        halo_send(f1, last, 1, hs.at[1], hr.at[2])
+        first_comps(lambda c: edges(f0, c, emit_rhs))
+        halo_send(f1, 0, last, hs.at[0], hr.at[1], ACROSS_X)
+        edges(f0, last, emit_rhs_t)
+        halo_send(f1, last, 1, hs.at[1], hr.at[2], ACROSS_X)
+        first_comps(lambda c: inside(f0, c, emit_rhs))
+        halo_send(f1, 0, last, hs.at[0], hr.at[1], ALONG_Y)
+        inside(f0, last, emit_rhs_t)
+        halo_send(f1, last, 1, hs.at[1], hr.at[2], ALONG_Y)
         for l in range(bpd):
             base[l] = -first_of(f1, l)
 
@@ -477,13 +511,15 @@
             gr_f[l] = gap
         pulled_send(2, 1, 1)
         wait_halo(hr.at[1], last)
-        first_comps(lambda c: apply(f1, c, emit_v1))
-        halo_send(f2, 0, last, hs.at[0], hr.at[3])
+        first_comps(lambda c: edges(f1, c, emit_v1))
+        halo_send(f2, 0, last, hs.at[0], hr.at[3], ACROSS_X)
         wait_halo(hr.at[2], 1)
-        apply(f1, last, emit_v1)
-        for l in range(bpd):
-            take_off(f2, l, t_f[l])
-        halo_send(f2, last, 1, hs.at[2], hr.at[4])
+        edges(f1, last, emit_v1_t)
+        halo_send(f2, last, 1, hs.at[2], hr.at[4], ACROSS_X)
+        first_comps(lambda c: inside(f1, c, emit_v1))
+        halo_send(f2, 0, last, hs.at[0], hr.at[3], ALONG_Y)
+        inside(f1, last, emit_v1_t)
+        halo_send(f2, last, 1, hs.at[2], hr.at[4], ALONG_Y)
         for l in range(bpd):
             base[l] = -first_of(f2, l)
         first_comps(dots)
@@ -491,8 +527,9 @@
         dots(last)
         pl.loop(0, comp)(near_dots)
         wait_halo(hr.at[3], last)
+        first_comps(lambda c: image_dots(c, False))
         wait_halo(hr.at[4], 1)
-        pl.loop(0, comp)(lambda c: image_dots(c, False))
+        image_dots(last, False)
 
         wait_rows(sr.at[2], ngx * bpd)
         if ngx > 1:

time: 25.2 us -> 24.8 us (0.984)
  Pallas kernels: 24.4 us -> 24 us
    pallas_call x1, Pallas kernels: 23.6 us -> 23.2 us  [on_device(): pl.pallas_call(functools.partial(kernel, nb, ngx, ngy), out_shape=(pltpu....]
where the time goes in v3:
time: 24.8 us; the launch traced here: 24.7 us
  Pallas kernels  24 us (97%)
  between operations  0.64 us (3%)
    pallas_call x1, Pallas kernels, on_device(): pl.pallas_call(functools.partial(kernel, nb, ngx, ngy), out_shape=(pltpu....  23.2 us
    pallas_call x1, Pallas kernels, on_device(): pl.pallas_call(out_kernel, out_shape=(jax.ShapeDtypeStruct(disp.shape, f3...  0.8 us

profile of v3, /device:TPU:0, one launch (start us, length us, event | category | flops | bytes accessed | tf_op | source)
XLA Modules:
  0.0 24.7 jit_solution(4630189359868937065)
XLA Ops:
  0.6 23.2 %newton_step.1 = (f32[3,8,32,128]{3,2,1,0:T(8,128)S(1)}, f32[3,8,32,128]{3,2,1,0:T(8,128)S(1)}, f32[8,128]{1,0:T(8,128)S(1)}, f32[3,2,1,128]{3,2,1,0:T(1,128)S(1)}) custom-call(f32[1,3,8,32,128]{4,3,2,1,0:T(8,128)} %disp.1, f32[1,3,8,32,128]{4,3,2,1,0:T(8,128)} %force.1, f32[1,8,32,128]{3,2,1,0:T(8,128)} %kappa.1, f32[1,8,32,128]{3,2,1,0:T(8,128)} %sigma.1, ...), custom_call_target="tpu_custom_call" | custom-call | tf_op jit(solution)/shard_map/newton_step/pallas_call | solution.py:637
  23.9 0.8 %newton_out.1 = (f32[1,3,8,32,128]{4,3,2,1,0:T(8,128)}, f32[2,128]{1,0:T(2,128)}) custom-call(f32[3,8,32,128]{3,2,1,0:T(8,128)S(1)} %get-tuple-element.6.r0, f32[3,8,32,128]{3,2,1,0:T(8,128)S(1)} %get-tuple-element.7.v1, f32[8,128]{1,0:T(8,128)S(1)} %get-tuple-element.8.coef, f32[3,2,1,128]{3,2,1,0:T(1,128)S(1)} %get-tuple-element.9.npr), custom_call_target="tpu_custom_call" | custom-call | tf_op jit(solution)/shard_map/newton_out/pallas_call | solution.py:671

commit v4 on v3

--- a/solution.py
+++ b/solution.py
@@ -400,13 +400,17 @@
         else:
             each_peer(lambda k: go(place_of(lax.rem(me + k, count))))
 
+    def first_surface():
+        wait_rows(ls.at[0], cx * cy)
+        surface_rows(f0, 0)
+
+    pl.when((b == 1) & (gx < ngx - 1))(first_surface)
     pl.semaphore_wait(barrier, expect)
     halo_send_args(CORNERS + ALONG_Y)
 
     @pl.when(b == 1)
     def _():
-        wait_rows(ls.at[0], cx * cy)
-        surface_rows(f0, 0)
+        pl.when(gx == ngx - 1)(first_surface)
         surf_send(0)
 
     halo_send_args(FACES_X)
@@ -584,7 +588,9 @@
     lanes = lax.broadcasted_iota(jnp.int32, (count, sblk), 1)
     sums = jnp.sum(table, axis=0, keepdims=True)
     norm0 = sums[:, RR : RR + 1]
-    alpha0 = norm0 / sums[:, RV : RV + 1]
+    product0 = sums[:, RV : RV + 1]
+    alpha0 = norm0 / product0
+    per_norm0 = 1.0 / norm0
     delta = alpha0 - table[:, OWN : OWN + 1]
 
     def pick(weights):
@@ -595,8 +601,8 @@
 
     norm1 = pick(((NN, 1.0), (NV, -2.0 * delta), (VV, delta * delta)))
     product1 = pick(((NV, 1.0), (VV, -delta), (NW, -alpha0), (VW, alpha0 * delta)))
-    ratio = norm1 / norm0
-    alpha1 = norm1 / (product1 - ratio * norm1 / alpha0)
+    ratio = norm1 * per_norm0
+    alpha1 = norm1 / (product1 - ratio * (ratio * product0))
     coef[0:1, :] = jnp.broadcast_to(alpha0 + alpha1 * (1.0 + ratio), (1, nz))
     coef[1:2, :] = jnp.broadcast_to(-alpha1 * alpha0, (1, nz))
 
@@ -606,15 +612,15 @@
     bpd = rows.shape[0]
     cr, cv = coef[0:1, :], coef[1:2, :]
     copies = []
+    for l in range(bpd):
+        rows[l : l + 1, :] = npr[0, l] - (cr * npr[1, l] + cv * npr[2, l])
+    copies.append(pltpu.make_async_copy(rows, new_press, sems.at[comp]))
+    copies[-1].start()
     for c in range(comp):
         for x in range(cx):
             buf[c, x] = cr * r0[c, x] + cv * v1[c, x]
         copies.append(pltpu.make_async_copy(buf.at[c], inc.at[0, c], sems.at[c]))
         copies[-1].start()
-    for l in range(bpd):
-        rows[l : l + 1, :] = npr[0, l] - (cr * npr[1, l] + cv * npr[2, l])
-    copies.append(pltpu.make_async_copy(rows, new_press, sems.at[comp]))
-    copies[-1].start()
     for copy in copies:
         copy.wait()
 

time: 24.8 us -> 24.8 us (level)
  no operation moved by 1% of the time
where the time goes in v4:
time: 24.8 us; the launch traced here: 24.7 us
  Pallas kernels  24 us (97%)
  between operations  0.64 us (3%)
    pallas_call x1, Pallas kernels, on_device(): pl.pallas_call(functools.partial(kernel, nb, ngx, ngy), out_shape=(pltpu....  23.2 us
    pallas_call x1, Pallas kernels, on_device(): pl.pallas_call(out_kernel, out_shape=(jax.ShapeDtypeStruct(disp.shape, f3...  0.8 us

profile of v4, /device:TPU:0, one launch (start us, length us, event | category | flops | bytes accessed | tf_op | source)
XLA Modules:
  0.0 24.7 jit_solution(13282641702559310104)
XLA Ops:
  0.6 23.2 %newton_step.1 = (f32[3,8,32,128]{3,2,1,0:T(8,128)S(1)}, f32[3,8,32,128]{3,2,1,0:T(8,128)S(1)}, f32[8,128]{1,0:T(8,128)S(1)}, f32[3,2,1,128]{3,2,1,0:T(1,128)S(1)}) custom-call(f32[1,3,8,32,128]{4,3,2,1,0:T(8,128)} %disp.1, f32[1,3,8,32,128]{4,3,2,1,0:T(8,128)} %force.1, f32[1,8,32,128]{3,2,1,0:T(8,128)} %kappa.1, f32[1,8,32,128]{3,2,1,0:T(8,128)} %sigma.1, ...), custom_call_target="tpu_custom_call" | custom-call | tf_op jit(solution)/shard_map/newton_step/pallas_call | solution.py:643
  23.9 0.8 %newton_out.1 = (f32[1,3,8,32,128]{4,3,2,1,0:T(8,128)}, f32[2,128]{1,0:T(2,128)}) custom-call(f32[3,8,32,128]{3,2,1,0:T(8,128)S(1)} %get-tuple-element.6.r0, f32[3,8,32,128]{3,2,1,0:T(8,128)S(1)} %get-tuple-element.7.v1, f32[8,128]{1,0:T(8,128)S(1)} %get-tuple-element.8.coef, f32[3,2,1,128]{3,2,1,0:T(1,128)S(1)} %get-tuple-element.9.npr), custom_call_target="tpu_custom_call" | custom-call | tf_op jit(solution)/shard_map/newton_out/pallas_call | solution.py:677

commit v5 on v4

--- a/solution.py
+++ b/solution.py
@@ -87,6 +87,11 @@
     barrier = pltpu.get_barrier_semaphore()
     if ngy <= 4:
         expect = jnp.where(b == 1, ngx, 0)
+        @pl.when(b == 0)
+        def _():
+            for k in reversed(range(ngx)):
+                pl.semaphore_signal(barrier, inc=1, device_id={"body": 1, "gx": far(gx, k, ngx)},
+                                    device_id_type=MESH)
         for dx, dy in DIRS:
             here = exists(dx, dy)
             expect = expect + as_int(here)
@@ -94,10 +99,6 @@
             @pl.when(here)
             def _():
                 pl.semaphore_signal(barrier, inc=1, device_id={"gx": gx + dx, "gy": gy + dy}, device_id_type=MESH)
-        for g in range(ngx):
-            @pl.when(b == 0)
-            def _():
-                pl.semaphore_signal(barrier, inc=1, device_id={"body": 1, "gx": g}, device_id_type=MESH)
     else:
         each_peer(lambda k: pl.semaphore_signal(barrier, inc=1, device_id=place_of(lax.rem(me + k, count)),
                                                 device_id_type=MESH))
@@ -364,8 +365,7 @@
             acc[k] = acc[k] + v
 
     def first_comps(act):
-        @pl.loop(0, last)
-        def _(c):
+        for c in range(last):
             act(c)
 
     def gap_of(l, s1):

time: 24.8 us -> 24.5 us (0.988)
  Pallas kernels: 24 us -> 23.7 us
    pallas_call x1, Pallas kernels: 23.2 us -> 22.9 us  [on_device(): pl.pallas_call(functools.partial(kernel, nb, ngx, ngy), out_shape=(pltpu....]
where the time goes in v5:
time: 24.5 us; the launch traced here: 24.4 us
  Pallas kernels  23.7 us (97%)
  between operations  0.64 us (3%)
    pallas_call x1, Pallas kernels, on_device(): pl.pallas_call(functools.partial(kernel, nb, ngx, ngy), out_shape=(pltpu....  22.9 us
    pallas_call x1, Pallas kernels, on_device(): pl.pallas_call(out_kernel, out_shape=(jax.ShapeDtypeStruct(disp.shape, f3...  0.8 us

profile of v5, /device:TPU:0, one launch (start us, length us, event | category | flops | bytes accessed | tf_op | source)
XLA Modules:
  0.0 24.4 jit_solution(9942924478236086749)
XLA Ops:
  0.6 22.9 %newton_step.1 = (f32[3,8,32,128]{3,2,1,0:T(8,128)S(1)}, f32[3,8,32,128]{3,2,1,0:T(8,128)S(1)}, f32[8,128]{1,0:T(8,128)S(1)}, f32[3,2,1,128]{3,2,1,0:T(1,128)S(1)}) custom-call(f32[1,3,8,32,128]{4,3,2,1,0:T(8,128)} %disp.1, f32[1,3,8,32,128]{4,3,2,1,0:T(8,128)} %force.1, f32[1,8,32,128]{3,2,1,0:T(8,128)} %kappa.1, f32[1,8,32,128]{3,2,1,0:T(8,128)} %sigma.1, ...), custom_call_target="tpu_custom_call" | custom-call | tf_op jit(solution)/shard_map/newton_step/pallas_call | solution.py:643
  23.6 0.8 %newton_out.1 = (f32[1,3,8,32,128]{4,3,2,1,0:T(8,128)}, f32[2,128]{1,0:T(2,128)}) custom-call(f32[3,8,32,128]{3,2,1,0:T(8,128)S(1)} %get-tuple-element.6.r0, f32[3,8,32,128]{3,2,1,0:T(8,128)S(1)} %get-tuple-element.7.v1, f32[8,128]{1,0:T(8,128)S(1)} %get-tuple-element.8.coef, f32[3,2,1,128]{3,2,1,0:T(1,128)S(1)} %get-tuple-element.9.npr), custom_call_target="tpu_custom_call" | custom-call | tf_op jit(solution)/shard_map/newton_out/pallas_call | solution.py:677
